TPU v7x, 32 devices: a whole 2x2x4 slice. The times are simulated.
32 devices in a mesh: level: 8 (over z, y), bal: 4 (over x, core).
Axes of the slice: x: 2, y: 2, z: 4, core: 2. Of those that a mesh axis runs over, the one named last changes fastest.
Arguments:
- patches: float32 [640, 5, 4096], P(('level', 'bal')), may hold values from -6 to 6
- patch_ids: int32 [640], P(('level', 'bal')), may hold values from 0 to 639, each once
- live: int32 [32], P(('level', 'bal')), may hold values from 4 to 12, as said below
- counts: int32 [2, 32], P(None, ('level', 'bal')), may hold values from 0 to 4, as said below
- parent_of: int32 [640], replicated, may hold values from 0 to 15
Outputs:
- new_patches: float32 [640, 5, 4096], P(('level', 'bal'))
- new_ids: int32 [640], P(('level', 'bal'))
- coarse: float32 [16, 5, 512], P('level')
Inputs may be any that keep to these rules, and one draw needn't show every extreme that they name: In every level group one device holds exactly 12 live patches. counts[r, d] never exceeds the live patches of device d at the start of round r; in every round and level group some device sends exactly 4.
All inputs are finite; a program needn't handle non-finite values.
Results may differ from a plain program's by a relative error of at most 0.0003.
Values sent between devices are 32-bit elements; how exact they have to be, the bound alone decides.
A program may use at most 64 MiB of HBM per device.

v0:
```python
import jax
import jax.numpy as jnp
from jax import lax
from jax.sharding import PartitionSpec as P

EDGE = 16
VARS = 5
SEND_MOST = 4
PAR_DEV = 2


def from_partner(array, axis, stride):
    return lax.ppermute(array, axis, [(i, i ^ 1 << stride) for i in range(lax.axis_size(axis))])


def restrict(fine_rows):
    leading = fine_rows.shape[:-1]
    half_edge = EDGE // 2
    blocks = fine_rows.reshape(leading + (half_edge, 2, half_edge, 2, half_edge, 2))
    return jnp.mean(blocks, axis=(-5, -3, -1)).reshape(
        leading + (half_edge * half_edge * half_edge,)
    )


def take_top(fine_rows, fine_ids, held_count, sent_count):
    capacity = fine_rows.shape[0]
    lane_index = jnp.arange(SEND_MOST, dtype=jnp.int32)
    pick_index = jnp.clip(held_count - sent_count + lane_index, 0, capacity - 1)
    is_valid = lane_index < sent_count
    return (
        jnp.where(is_valid[:, None, None], fine_rows[pick_index], 0.0),
        jnp.where(is_valid, fine_ids[pick_index], -1),
    )


def place_rows(fine_rows, fine_ids, kept_count, in_rows, in_ids):
    capacity = fine_rows.shape[0]
    slot_index = jnp.arange(capacity, dtype=jnp.int32)
    offset = slot_index - kept_count
    is_hit = (offset >= 0) & (offset < SEND_MOST)
    place_index = jnp.clip(offset, 0, SEND_MOST - 1)
    is_kept = slot_index < kept_count
    new_rows = jnp.where(
        is_kept[:, None, None],
        fine_rows,
        jnp.where(is_hit[:, None, None], in_rows[place_index], 0.0),
    )
    new_ids = jnp.where(is_kept, fine_ids, jnp.where(is_hit, in_ids[place_index], -1))
    return (new_rows, new_ids)


def pairwise_move(fine_rows, fine_ids, held_count, counts, rounds):
    for turn_index in range(rounds):
        sent_count = counts[turn_index, 0]
        out_rows, out_ids = take_top(fine_rows, fine_ids, held_count, sent_count)
        in_rows, in_marks = from_partner((out_rows, out_ids.astype(jnp.float32)), "bal", turn_index)
        in_ids = in_marks.astype(jnp.int32)
        kept_count = held_count - sent_count
        fine_rows, fine_ids = place_rows(fine_rows, fine_ids, kept_count, in_rows, in_ids)
        held_count = kept_count + jnp.sum((in_ids >= 0).astype(jnp.int32))
    return (fine_rows, fine_ids)


def parent_sums(fine_rows, fine_ids, parent_of):
    capacity = fine_rows.shape[0]
    reduced = restrict(fine_rows).reshape(capacity, -1)
    parent = jnp.where(fine_ids >= 0, parent_of[jnp.clip(fine_ids, 0, parent_of.shape[0] - 1)], -1)
    wanted = jnp.arange(lax.axis_size("level") * PAR_DEV, dtype=jnp.int32)
    one_hot = (wanted[:, None] == parent[None, :]).astype(jnp.float32)
    level_sums = lax.psum_scatter(
        jnp.dot(one_hot, reduced, precision=lax.Precision.HIGHEST),
        "level",
        scatter_dimension=0,
        tiled=True,
    )
    group_sums = lax.psum(level_sums, "bal")
    return group_sums.reshape(PAR_DEV, VARS, -1)


def per_device(patches, patch_ids, live, counts, parent_of):
    capacity = patches.shape[0]
    group = lax.axis_size("bal")
    rounds = group.bit_length() - 1
    slot_index = jnp.arange(capacity, dtype=jnp.int32)
    held_count = live[0]
    is_kept = slot_index < held_count
    fine_rows = jnp.where(is_kept[:, None, None], patches, 0.0)
    fine_ids = jnp.where(is_kept, patch_ids, -1)
    coarse = parent_sums(fine_rows, fine_ids, parent_of)
    fine_rows, fine_ids = pairwise_move(fine_rows, fine_ids, held_count, counts, rounds)
    return (fine_rows, fine_ids, coarse)


def solution(mesh):
    return jax.shard_map(
        per_device,
        mesh=mesh,
        in_specs=(
            P(("level", "bal"), None, None),
            P(("level", "bal")),
            P(("level", "bal")),
            P(None, ("level", "bal")),
            P(),
        ),
        out_specs=(P(("level", "bal"), None, None), P(("level", "bal")), P("level", None, None)),
        check_vma=False,
    )
```

profile of v0, /device:TPU:0, one launch (start us, length us, event | category | flops | bytes accessed | tf_op | source)
XLA Modules:
  0.0 143.0 jit_solution(11142344460428278387)
XLA Ops:
  7.2 0.0 copy-start
  7.2 0.0 all-reduce.3.cloned.1.call-start
  7.2 1.3 fusion.13
  9.2 0.6 iota_compare_fusion.5
  10.4 0.0 copy-start.1
  10.4 2.7 %copy_select_fusion = f32[20,5,4096]{2,1,0:T(8,128)S(1)} fusion(f32[20,5,4096]{2,0,1:T(8,128)} %param.5, pred[20]{0:T(512)(128)(4,1)S(1)} %iota_compare_fusion.4), kind=kLoop, calls=%fused_computation.7 | loop fusion | flops 409600 | bytes 3276820 | tf_op jit(solution)/shard_map/jit(_where)/select_n | solution.py:87
  13.1 0.6 gather_fusion.1
  13.7 0.9 broadcast_select_fusion.1
  14.6 0.5 collective-permute-start.1
  15.1 0.0 copy-done.1
  15.1 0.6 gather_fusion
  15.7 0.6 select_convert_fusion.1
  16.3 0.1 collective-permute-start
  16.4 6.2 %copy.14 = f32[20,5,4096]{0,2,1:T(8,128)} copy(f32[20,5,4096]{2,1,0:T(8,128)S(1)} %copy_select_fusion) | data formatting | bytes 3276800 | tf_op jit(solution)/shard_map/jit(_where)/select_n | solution.py:87
  22.6 0.6 iota_compare_fusion.2
  23.3 10.6 %reduce_sum.19 = f32[20,5,8,8,8]{0,4,3,2,1:T(8,128)S(1)} reduce(f32[20,5,8,2,8,2,8,2]{0,7,6,5,4,3,2,1:T(2,128)} %bitcast.30, f32[]{:T(128)} %constant.3.clone.1), dimensions={3,5,7}, to_apply=%region_1.2 | reduce | flops 358400 | bytes 1843204 | tf_op jit(solution)/shard_map/reduce_sum | solution.py:20
  33.9 0.0 copy-start.2
  33.9 0.2 broadcast_multiply_fusion
  34.1 0.0 copy-done
  34.1 0.7 gather_fusion.6
  34.7 0.0 copy-done.2
  34.7 0.6 dynamic-slice
  36.0 0.0 collective-permute-done
  36.0 0.6 fusion.6
  38.0 0.7 fusion.12
  38.7 2.5 %compare_select_fusion.11 = (s32[20]{0:T(128)S(1)}, s32[20]{0:T(128)S(1)}) fusion(s32[20]{0:T(128)S(1)} %gather_fusion.6, s32[20]{0:T(128)S(1)} %get-tuple-element.10, s32[]{:T(128)} %bitcast.10, s32[]{:T(128)} %bitcast.9, s32[]{:T(128)} %bitcast.8, s32[]{:T(128)} %bitcast.7, s32[]{:T(128)S(6)} %sub.42), kind=kLoop, calls=%fused_computation.32 | loop fusion | flops 400 | bytes 340 | tf_op jit(solution)/shard_map/jit(_where)/select_n | solution.py:67
  41.2 0.6 gather_fusion.5
  41.8 0.7 select_convert_fusion
  42.5 3.0 %collective-permute-start.3 = (f32[4]{0:T(128)S(1)}, f32[4]{0:T(128)S(1)}, u32[]{:S(2)}, u32[]{:S(2)}) collective-permute-start(f32[4]{0:T(128)S(1)} %select_convert_fusion), channel_id=1, source_target_pairs={{0,2},{1,3},{2,0},{3,1},{4,6},{5,7},{6,4},{7,5},{8,10},{9,11},{10,... | collective-permute-start | bytes 56 | tf_op jit(solution)/shard_map/ppermute | solution.py:13
  45.5 1.4 fusion
  46.9 0.0 all-reduce.3.cloned.1.call-update
  46.9 0.1 collective-permute-done.3
  47.0 0.7 fusion.11
  47.7 3.0 %fusion.5 = s32[20]{0:T(128)} fusion(s32[20]{0:T(128)S(1)} %get-tuple-element.12, s32[]{:T(128)} %bitcast.11, s32[]{:T(128)} %bitcast.12, s32[]{:T(128)} %bitcast.13, s32[]{:T(128)} %bitcast.14, s32[]{:T(128)S(6)} %sub.43), kind=kLoop, calls=%fused_computation.39 | loop fusion | flops 360 | bytes 180 | tf_op jit(solution)/shard_map/jit(_where)/select_n | solution.py:48
  50.7 0.0 collective-permute-done.1
  50.7 2.2 %gather_fusion.2 = f32[20,5,4096]{2,1,0:T(8,128)} fusion(f32[4,5,4096]{2,1,0:T(8,128)S(1)} %collective-permute-done.1, s32[1024]{0:T(1024)S(1)} %pad_clamp_fusion.3), kind=kCustom, calls=%fused_computation.2 | custom fusion | bytes 3276880 | tf_op jit(solution)/shard_map/gather | solution.py:46
  52.9 3.8 %select_select_fusion.1 = f32[20,5,4096]{2,1,0:T(8,128)S(1)} fusion(f32[20,5,4096]{2,1,0:T(8,128)} %gather_fusion.2, pred[20]{0:T(512)(128)(4,1)S(1)} %get-tuple-element.23, pred[20]{0:T(512)(128)(4,1)S(1)} %get-tuple-element.24, f32[20,5,4096]{2,0,1:T(8,128)} %param.5, pred[20]{0:T(512)(128)(4,1)S(1)} %iota_compare_fusion.4), kind=kLoop, calls=%fused_computation.9 | loop fusion | flops 1228800 | bytes 4915260 | tf_op jit(solution)/shard_map/jit(_where)/select_n | solution.py:43
  56.8 0.6 gather_fusion.3
  57.3 0.9 broadcast_select_fusion
  58.2 2.0 %collective-permute-start.2 = (f32[4,5,4096]{2,1,0:T(8,128)}, f32[4,5,4096]{2,1,0:T(8,128)S(1)}, u32[]{:S(2)}, u32[]{:S(2)}) collective-permute-start(f32[4,5,4096]{2,1,0:T(8,128)} %broadcast_select_fusion), channel_id=1, source_target_pairs={{0,2},{1,3},{2,0},{3,1},{4,6},{5,7},{6,4},{7,5},{8,10},{9,11},{10,... | collective-permute-start | bytes 983048 | tf_op jit(solution)/shard_map/ppermute | solution.py:13
  60.3 57.1 %all-reduce.3.cloned.1.call-done = f32[16,2560]{1,0:T(8,128)} async-done(((f32[16,2560]{1,0:T(8,128)}), f32[16,2560]{1,0:T(8,128)}) %all-reduce.3.cloned.1.call-update) | async-done | bytes 163856
  117.4 0.9 constant_dynamic-slice_fusion
  118.3 10.3 %psum.7 = f32[2,5,512]{2,1,0:T(8,128)S(1)} all-reduce(f32[2,5,512]{2,1,0:T(8,128)S(1)} %reshape.127), channel_id=1, replica_groups=mesh['level'=8,'bal'=4] {'bal'}, use_global_device_ids=true, to_apply=%region_3.4 | all-reduce | flops 5120 | bytes 40960 | tf_op jit(solution)/shard_map/psum | solution.py:76
  128.6 0.6 copy.16
  129.2 0.0 collective-permute-done.2
  129.2 2.2 %gather_fusion.4 = f32[20,5,4096]{2,1,0:T(8,128)} fusion(f32[4,5,4096]{2,1,0:T(8,128)S(1)} %collective-permute-done.2, s32[1024]{0:T(1024)S(1)} %pad_clamp_fusion.1), kind=kCustom, calls=%fused_computation.4 | custom fusion | bytes 3276880 | tf_op jit(solution)/shard_map/gather | solution.py:46
  131.5 2.4 %select_select_fusion = f32[20,5,4096]{2,1,0:T(8,128)S(1)} fusion(f32[20,5,4096]{2,1,0:T(8,128)S(1)} %select_select_fusion.1, f32[20,5,4096]{2,1,0:T(8,128)} %gather_fusion.4, pred[20]{0:T(512)(128)(4,1)S(1)} %get-tuple-element.25, pred[20]{0:T(512)(128)(4,1)S(1)} %get-tuple-element.26), kind=kLoop, calls=%fused_computation.8 | loop fusion | flops 819200 | bytes 4915240 | tf_op jit(solution)/shard_map/jit(_where)/select_n | solution.py:43
  133.9 2.2 %copy.15 = f32[20,5,4096]{2,0,1:T(8,128)} copy(f32[20,5,4096]{2,1,0:T(8,128)S(1)} %select_select_fusion) | data formatting | bytes 3276800
  (16 shorter events, 0.1 us)
Async XLA Ops:
  7.2 26.9 %copy-start = (s32[640]{0:T(1024)S(1)}, s32[640]{0:T(1024)}, u32[]{:S(2)}) copy-start(s32[640]{0:T(1024)} %param.9) | copy-start | bytes 7684
  7.2 110.2 %all-reduce.3.cloned.1.call-start = ((), (), s32[]{:S(2)}) async-start(), calls=%async_computation | async-start | bytes 327680
  10.4 4.7 %copy-start.1 = (s32[20]{0:T(128)S(1)}, s32[20]{0:T(128)}, u32[]{:S(2)}) copy-start(s32[20]{0:T(128)} %param.6) | copy-start | bytes 244
  14.6 36.1 %collective-permute-start.1 = (f32[4,5,4096]{2,1,0:T(8,128)}, f32[4,5,4096]{2,1,0:T(8,128)S(1)}, u32[]{:S(2)}, u32[]{:S(2)}) collective-permute-start(f32[4,5,4096]{2,1,0:T(8,128)} %broadcast_select_fusion.1), channel_id=1, source_target_pairs={{0,1},{1,0},{2,3},{3,2},{4,5},{5,4},{6,7},{7,6},{8,9},{9,8},{10,11... | collective-permute-start | bytes 983048 | tf_op jit(solution)/shard_map/ppermute | solution.py:13
  16.3 19.7 %collective-permute-start = (f32[4]{0:T(128)S(1)}, f32[4]{0:T(128)S(1)}, u32[]{:S(2)}, u32[]{:S(2)}) collective-permute-start(f32[4]{0:T(128)S(1)} %select_convert_fusion.1), channel_id=1, source_target_pairs={{0,1},{1,0},{2,3},{3,2},{4,5},{5,4},{6,7},{7,6},{8,9},{9,8},{10,11... | collective-permute-start | bytes 56 | tf_op jit(solution)/shard_map/ppermute | solution.py:13
  33.9 0.9 copy-start.2
  42.5 4.6 %collective-permute-start.3 = (f32[4]{0:T(128)S(1)}, f32[4]{0:T(128)S(1)}, u32[]{:S(2)}, u32[]{:S(2)}) collective-permute-start(f32[4]{0:T(128)S(1)} %select_convert_fusion), channel_id=1, source_target_pairs={{0,2},{1,3},{2,0},{3,1},{4,6},{5,7},{6,4},{7,5},{8,10},{9,11},{10,... | collective-permute-start | bytes 56 | tf_op jit(solution)/shard_map/ppermute | solution.py:13
  58.2 71.0 %collective-permute-start.2 = (f32[4,5,4096]{2,1,0:T(8,128)}, f32[4,5,4096]{2,1,0:T(8,128)S(1)}, u32[]{:S(2)}, u32[]{:S(2)}) collective-permute-start(f32[4,5,4096]{2,1,0:T(8,128)} %broadcast_select_fusion), channel_id=1, source_target_pairs={{0,2},{1,3},{2,0},{3,1},{4,6},{5,7},{6,4},{7,5},{8,10},{9,11},{10,... | collective-permute-start | bytes 983048 | tf_op jit(solution)/shard_map/ppermute | solution.py:13
Sparse Core Ops, SparseCore 0:
  47.0 70.3 all-reduce.2
where the time goes:
time: 144 us; the launch traced here: 143 us
  waiting for transfers between devices  57.3 us (40%)
  other arithmetic  30.1 us (21%)
  local copies, waits for them, and re-layouts  20.8 us (14%)
  between operations  17.4 us (12%)
  blocking collectives  10.3 us (7%)
  starting transfers between devices  5.65 us (4%)
    unnamed x2, waiting for transfers between devices  57.2 us
    reduce_sum x1, other arithmetic, restrict(): jnp.mean(blocks, axis=(-5, -3, -1))  10.6 us
    psum x1, blocking collectives, parent_sums(): group_sums = lax.psum(level_sums, 'bal')  10.3 us
    select_n x2, other arithmetic, place_rows(): jnp.where(is_kept[:, None, None], fine_rows, jnp.where(is_hit[:, None, No...  6.28 us
    select_n x1, local copies, waits for them, and re-layouts, per_device(): fine_rows = jnp.where(is_kept[:, None, None], patches, 0.0)  6.24 us
    ppermute x4, starting transfers between devices, from_partner(): lax.ppermute(array, axis, [(i, i ^ 1 << stride) for i in range(lax.axis_s...  5.62 us
    gather x2, local copies, waits for them, and re-layouts, place_rows(): in_rows[place_index]  4.45 us
    unnamed x10, local copies, waits for them, and re-layouts  4.34 us
  transfers between devices with their start and end apart: 5, of which 2 were waited for; matrix products, arithmetic and copies ran while one was open for 28% of the time, Pallas kernels for 0%

commit v1 on v0

--- a/solution.py
+++ b/solution.py
@@ -73,7 +73,7 @@
         scatter_dimension=0,
         tiled=True,
     )
-    group_sums = lax.psum(level_sums, "bal")
+    group_sums = jnp.sum(lax.all_gather(level_sums, "bal"), axis=0)
     return group_sums.reshape(PAR_DEV, VARS, -1)
 
 

time: 144 us -> 139 us (0.965)
  blocking collectives: 10.3 us -> 5.28 us
    psum x1 -> x0, blocking collectives: 10.3 us -> none  [parent_sums(): group_sums = lax.psum(level_sums, 'bal')]
    all_gather x0 -> x1, blocking collectives: none -> 5.28 us  [parent_sums(): group_sums = jnp.sum(lax.all_gather(level_sums, 'bal'), axis=0)]
    unnamed x10 -> x9, local copies, waits for them, and re-layouts: 4.34 us -> 3.72 us
  transfers between devices with their start and end apart: 5 -> 5, of which waited for: 2 -> 2; matrix products, arithmetic and copies ran while one was open for 28% -> 29% of each run, Pallas kernels for 0% -> 0%
where the time goes in v1:
time: 139 us; the launch traced here: 138 us
  waiting for transfers between devices  57.3 us (41%)
  other arithmetic  30.7 us (22%)
  local copies, waits for them, and re-layouts  20.2 us (15%)
  between operations  17.4 us (13%)
  starting transfers between devices  5.65 us (4%)
  blocking collectives  5.28 us (4%)
  matrix products  1.41 us (1%)
    unnamed x2, waiting for transfers between devices  57.2 us
    reduce_sum x1, other arithmetic, restrict(): jnp.mean(blocks, axis=(-5, -3, -1))  10.6 us
    select_n x2, other arithmetic, place_rows(): jnp.where(is_kept[:, None, None], fine_rows, jnp.where(is_hit[:, None, No...  6.28 us
    select_n x1, local copies, waits for them, and re-layouts, per_device(): fine_rows = jnp.where(is_kept[:, None, None], patches, 0.0)  6.24 us
    ppermute x4, starting transfers between devices, from_partner(): lax.ppermute(array, axis, [(i, i ^ 1 << stride) for i in range(lax.axis_s...  5.62 us
    all_gather x1, blocking collectives, parent_sums(): group_sums = jnp.sum(lax.all_gather(level_sums, 'bal'), axis=0)  5.28 us
    gather x2, local copies, waits for them, and re-layouts, place_rows(): in_rows[place_index]  4.45 us
    unnamed x9, local copies, waits for them, and re-layouts  3.72 us
  transfers between devices with their start and end apart: 5, of which 2 were waited for; matrix products, arithmetic and copies ran while one was open for 29% of the time, Pallas kernels for 0%

profile of v1, /device:TPU:0, one launch (start us, length us, event | category | flops | bytes accessed | tf_op | source)
XLA Modules:
  0.0 138.0 jit_solution(9068475344349914477)
XLA Ops:
  7.2 0.0 copy-start
  7.2 0.0 all-reduce.3.cloned.1.call-start
  7.2 1.3 fusion.13
  9.2 0.6 iota_compare_fusion.5
  10.4 0.0 copy-start.1
  10.4 2.7 %copy_select_fusion = f32[20,5,4096]{2,1,0:T(8,128)S(1)} fusion(f32[20,5,4096]{2,0,1:T(8,128)} %param.5, pred[20]{0:T(512)(128)(4,1)S(1)} %iota_compare_fusion.4), kind=kLoop, calls=%fused_computation.7 | loop fusion | flops 409600 | bytes 3276820 | tf_op jit(solution)/shard_map/jit(_where)/select_n | solution.py:87
  13.1 0.6 gather_fusion.1
  13.7 0.9 broadcast_select_fusion.1
  14.6 0.5 collective-permute-start.1
  15.1 0.0 copy-done.1
  15.1 0.6 gather_fusion
  15.7 0.6 select_convert_fusion.1
  16.3 0.1 collective-permute-start
  16.4 6.2 %copy.12 = f32[20,5,4096]{0,2,1:T(8,128)} copy(f32[20,5,4096]{2,1,0:T(8,128)S(1)} %copy_select_fusion) | data formatting | bytes 3276800 | tf_op jit(solution)/shard_map/jit(_where)/select_n | solution.py:87
  22.6 0.6 iota_compare_fusion.2
  23.3 10.6 %reduce_sum.28 = f32[20,5,8,8,8]{0,4,3,2,1:T(8,128)S(1)} reduce(f32[20,5,8,2,8,2,8,2]{0,7,6,5,4,3,2,1:T(2,128)} %bitcast.33, f32[]{:T(128)} %constant.3.clone.1), dimensions={3,5,7}, to_apply=%region_1.2 | reduce | flops 358400 | bytes 1843204 | tf_op jit(solution)/shard_map/reduce_sum | solution.py:20
  33.9 0.0 copy-start.2
  33.9 0.2 broadcast_multiply_fusion
  34.1 0.0 copy-done
  34.1 0.7 gather_fusion.6
  34.7 0.0 copy-done.2
  34.7 0.6 dynamic-slice
  36.0 0.0 collective-permute-done
  36.0 0.6 fusion.6
  38.0 0.7 fusion.12
  38.7 2.5 %compare_select_fusion.11 = (s32[20]{0:T(128)S(1)}, s32[20]{0:T(128)S(1)}) fusion(s32[20]{0:T(128)S(1)} %gather_fusion.6, s32[20]{0:T(128)S(1)} %get-tuple-element.10, s32[]{:T(128)} %bitcast.10, s32[]{:T(128)} %bitcast.9, s32[]{:T(128)} %bitcast.8, s32[]{:T(128)} %bitcast.7, s32[]{:T(128)S(6)} %sub.42), kind=kLoop, calls=%fused_computation.33 | loop fusion | flops 400 | bytes 340 | tf_op jit(solution)/shard_map/jit(_where)/select_n | solution.py:67
  41.2 0.6 gather_fusion.5
  41.8 0.7 select_convert_fusion
  42.5 3.0 %collective-permute-start.3 = (f32[4]{0:T(128)S(1)}, f32[4]{0:T(128)S(1)}, u32[]{:S(2)}, u32[]{:S(2)}) collective-permute-start(f32[4]{0:T(128)S(1)} %select_convert_fusion), channel_id=1, source_target_pairs={{0,2},{1,3},{2,0},{3,1},{4,6},{5,7},{6,4},{7,5},{8,10},{9,11},{10,... | collective-permute-start | bytes 56 | tf_op jit(solution)/shard_map/ppermute | solution.py:13
  45.5 1.4 %fusion = f32[16,2560]{1,0:T(8,128)} fusion(f32[20,2560]{0,1:T(8,128)S(1)} %bitcast.34, s32[20]{0:T(128)S(1)} %get-tuple-element.11), kind=kOutput, calls=%fused_computation.15 | convolution fusion | flops 9830720 | bytes 368720 | tf_op jit(solution)/shard_map/dot_general | solution.py:71
  46.9 0.0 all-reduce.3.cloned.1.call-update
  46.9 0.1 collective-permute-done.3
  47.0 0.7 fusion.11
  47.7 3.0 %fusion.5 = s32[20]{0:T(128)} fusion(s32[20]{0:T(128)S(1)} %get-tuple-element.12, s32[]{:T(128)} %bitcast.11, s32[]{:T(128)} %bitcast.12, s32[]{:T(128)} %bitcast.13, s32[]{:T(128)} %bitcast.14, s32[]{:T(128)S(6)} %sub.43), kind=kLoop, calls=%fused_computation.40 | loop fusion | flops 360 | bytes 180 | tf_op jit(solution)/shard_map/jit(_where)/select_n | solution.py:48
  50.7 0.0 collective-permute-done.1
  50.7 2.2 %gather_fusion.2 = f32[20,5,4096]{2,1,0:T(8,128)} fusion(f32[4,5,4096]{2,1,0:T(8,128)S(1)} %collective-permute-done.1, s32[1024]{0:T(1024)S(1)} %pad_clamp_fusion.3), kind=kCustom, calls=%fused_computation.2 | custom fusion | bytes 3276880 | tf_op jit(solution)/shard_map/gather | solution.py:46
  52.9 3.8 %select_select_fusion.1 = f32[20,5,4096]{2,1,0:T(8,128)S(1)} fusion(f32[20,5,4096]{2,1,0:T(8,128)} %gather_fusion.2, pred[20]{0:T(512)(128)(4,1)S(1)} %get-tuple-element.23, pred[20]{0:T(512)(128)(4,1)S(1)} %get-tuple-element.24, f32[20,5,4096]{2,0,1:T(8,128)} %param.5, pred[20]{0:T(512)(128)(4,1)S(1)} %iota_compare_fusion.4), kind=kLoop, calls=%fused_computation.9 | loop fusion | flops 1228800 | bytes 4915260 | tf_op jit(solution)/shard_map/jit(_where)/select_n | solution.py:43
  56.8 0.6 gather_fusion.3
  57.3 0.9 broadcast_select_fusion
  58.2 2.0 %collective-permute-start.2 = (f32[4,5,4096]{2,1,0:T(8,128)}, f32[4,5,4096]{2,1,0:T(8,128)S(1)}, u32[]{:S(2)}, u32[]{:S(2)}) collective-permute-start(f32[4,5,4096]{2,1,0:T(8,128)} %broadcast_select_fusion), channel_id=1, source_target_pairs={{0,2},{1,3},{2,0},{3,1},{4,6},{5,7},{6,4},{7,5},{8,10},{9,11},{10,... | collective-permute-start | bytes 983048 | tf_op jit(solution)/shard_map/ppermute | solution.py:13
  60.3 57.1 %all-reduce.3.cloned.1.call-done = f32[16,2560]{1,0:T(8,128)} async-done(((f32[16,2560]{1,0:T(8,128)}), f32[16,2560]{1,0:T(8,128)}) %all-reduce.3.cloned.1.call-update) | async-done | bytes 163856
  117.4 0.9 dynamic-slice_bitcast_fusion
  118.3 5.3 %all-gather.1 = f32[4,2,2560]{2,1,0:T(2,128)S(1)} all-gather(f32[1,2,2560]{2,1,0:T(2,128)S(1)} %dynamic-slice_bitcast_fusion), channel_id=2, replica_groups=mesh['level'=8,'bal'=4] {'bal'}, dimensions={0}, use_global_device_ids=true | all-gather | bytes 102400 | tf_op jit(solution)/shard_map/all_gather | solution.py:76
  123.6 0.6 reduce_sum.29
  124.2 0.0 collective-permute-done.2
  124.2 2.2 %gather_fusion.4 = f32[20,5,4096]{2,1,0:T(8,128)} fusion(f32[4,5,4096]{2,1,0:T(8,128)S(1)} %collective-permute-done.2, s32[1024]{0:T(1024)S(1)} %pad_clamp_fusion.1), kind=kCustom, calls=%fused_computation.4 | custom fusion | bytes 3276880 | tf_op jit(solution)/shard_map/gather | solution.py:46
  126.5 2.4 %select_select_fusion = f32[20,5,4096]{2,1,0:T(8,128)S(1)} fusion(f32[20,5,4096]{2,1,0:T(8,128)S(1)} %select_select_fusion.1, f32[20,5,4096]{2,1,0:T(8,128)} %gather_fusion.4, pred[20]{0:T(512)(128)(4,1)S(1)} %get-tuple-element.25, pred[20]{0:T(512)(128)(4,1)S(1)} %get-tuple-element.26), kind=kLoop, calls=%fused_computation.8 | loop fusion | flops 819200 | bytes 4915240 | tf_op jit(solution)/shard_map/jit(_where)/select_n | solution.py:43
  128.9 2.2 %copy.13 = f32[20,5,4096]{2,0,1:T(8,128)} copy(f32[20,5,4096]{2,1,0:T(8,128)S(1)} %select_select_fusion) | data formatting | bytes 3276800
  (15 shorter events, 0.1 us)
Async XLA Ops:
  7.2 26.9 %copy-start = (s32[640]{0:T(1024)S(1)}, s32[640]{0:T(1024)}, u32[]{:S(2)}) copy-start(s32[640]{0:T(1024)} %param.9) | copy-start | bytes 7684
  7.2 110.2 %all-reduce.3.cloned.1.call-start = ((), (), s32[]{:S(2)}) async-start(), calls=%async_computation | async-start | bytes 327680
  10.4 4.7 %copy-start.1 = (s32[20]{0:T(128)S(1)}, s32[20]{0:T(128)}, u32[]{:S(2)}) copy-start(s32[20]{0:T(128)} %param.6) | copy-start | bytes 244
  14.6 36.1 %collective-permute-start.1 = (f32[4,5,4096]{2,1,0:T(8,128)}, f32[4,5,4096]{2,1,0:T(8,128)S(1)}, u32[]{:S(2)}, u32[]{:S(2)}) collective-permute-start(f32[4,5,4096]{2,1,0:T(8,128)} %broadcast_select_fusion.1), channel_id=1, source_target_pairs={{0,1},{1,0},{2,3},{3,2},{4,5},{5,4},{6,7},{7,6},{8,9},{9,8},{10,11... | collective-permute-start | bytes 983048 | tf_op jit(solution)/shard_map/ppermute | solution.py:13
  16.3 19.7 %collective-permute-start = (f32[4]{0:T(128)S(1)}, f32[4]{0:T(128)S(1)}, u32[]{:S(2)}, u32[]{:S(2)}) collective-permute-start(f32[4]{0:T(128)S(1)} %select_convert_fusion.1), channel_id=1, source_target_pairs={{0,1},{1,0},{2,3},{3,2},{4,5},{5,4},{6,7},{7,6},{8,9},{9,8},{10,11... | collective-permute-start | bytes 56 | tf_op jit(solution)/shard_map/ppermute | solution.py:13
  33.9 0.9 copy-start.2
  42.5 4.6 %collective-permute-start.3 = (f32[4]{0:T(128)S(1)}, f32[4]{0:T(128)S(1)}, u32[]{:S(2)}, u32[]{:S(2)}) collective-permute-start(f32[4]{0:T(128)S(1)} %select_convert_fusion), channel_id=1, source_target_pairs={{0,2},{1,3},{2,0},{3,1},{4,6},{5,7},{6,4},{7,5},{8,10},{9,11},{10,... | collective-permute-start | bytes 56 | tf_op jit(solution)/shard_map/ppermute | solution.py:13
  58.2 66.0 %collective-permute-start.2 = (f32[4,5,4096]{2,1,0:T(8,128)}, f32[4,5,4096]{2,1,0:T(8,128)S(1)}, u32[]{:S(2)}, u32[]{:S(2)}) collective-permute-start(f32[4,5,4096]{2,1,0:T(8,128)} %broadcast_select_fusion), channel_id=1, source_target_pairs={{0,2},{1,3},{2,0},{3,1},{4,6},{5,7},{6,4},{7,5},{8,10},{9,11},{10,... | collective-permute-start | bytes 983048 | tf_op jit(solution)/shard_map/ppermute | solution.py:13
Sparse Core Ops, SparseCore 0:
  47.0 70.3 all-reduce.2
